TPU v7x, 32 devices: a whole 2x2x4 slice. The times are simulated.
32 devices in a mesh: dp: 8 (over y, x, core), tensor: 4 (over z).
Axes of the slice: x: 2, y: 2, z: 4, core: 2. Of those that a mesh axis runs over, the one named last changes fastest.
Arguments:
- tokens: bfloat16 [3072, 8192], P('dp', 'tensor'), may hold values from -6 to 6
- up_first: bfloat16 [16, 512, 512], P('tensor'), may hold values from -0.25 to 0.25
- up_second: bfloat16 [16, 512, 2048], P('tensor'), may hold values from -0.25 to 0.25
- down_first: bfloat16 [16, 2048, 512], P('tensor'), may hold values from -0.125 to 0.125
- down_second: bfloat16 [16, 512, 512], P('tensor'), may hold values from -0.25 to 0.25
- cotangent: bfloat16 [3072, 8192], P('dp', 'tensor'), may hold values from -6 to 6
Outputs:
- layer_out: bfloat16 [3072, 8192], P('dp', 'tensor')
- grad_tokens: bfloat16 [3072, 8192], P('dp', 'tensor')
- grad_up_first: float32 [16, 512, 512], P('tensor', 'dp')
- grad_up_second: float32 [16, 512, 2048], P('tensor', 'dp')
- grad_down_first: float32 [16, 2048, 512], P('tensor', 'dp')
- grad_down_second: float32 [16, 512, 512], P('tensor', 'dp')
All inputs are finite; a program needn't handle non-finite values.
Results may differ from a plain program's by a relative error of at most 0.023.
Values may be sent and summed in bfloat16 or wider, within the bound.
No kernel may reach another device: no remote copies, remote signals or barrier semaphores. Data moves between devices by JAX's collectives and lax.ppermute only.
A program may use at most 128 MiB of HBM per device.

v0:
```python
import jax
import jax.numpy as jnp
from jax import lax
from jax.sharding import PartitionSpec as P

NB = 16
gelu_coeff = 0.7978845608028654
cubic_coeff = 0.044715


def gelu_pair(hidden):
    inner_arg = gelu_coeff * (hidden + cubic_coeff * hidden * hidden * hidden)
    tangent = jnp.tanh(inner_arg)
    gelu_value = 0.5 * hidden * (1.0 + tangent)
    gelu_slope = 0.5 * (1.0 + tangent) + 0.5 * hidden * (1.0 - tangent * tangent) * gelu_coeff * (
        1.0 + 3.0 * cubic_coeff * hidden * hidden
    )
    return (gelu_value, gelu_slope)


def regroup(sliced, apply_fn):
    return apply_fn(lax.all_to_all(sliced, "tensor", split_axis=2, concat_axis=0, tiled=True))


def body(tokens, up_first, up_second, down_first, down_second, cotangent):
    token_rows = tokens.shape[0]
    local_blocks = up_first.shape[0]
    block_size = up_first.shape[1]
    hidden_size = up_second.shape[2]
    slice_width = block_size // NB
    data_count = lax.axis_size("dp")
    grad_scale = (token_rows * data_count) ** (-0.5)
    x_three = tokens.reshape(token_rows, local_blocks, block_size)
    up_four = up_first.reshape(local_blocks, block_size, NB, slice_width)
    mixed_up = jnp.einsum(
        "tbi,bijc->bcjt", x_three, up_four, preferred_element_type=jnp.float32
    ).astype(jnp.bfloat16)

    def lift_up(received):
        regrouped = received.reshape(block_size, local_blocks, received.shape[3])
        return (
            regrouped,
            jnp.einsum("mjt,jmo->jot", regrouped, up_second, preferred_element_type=jnp.float32),
        )

    regrouped_up, pre_act = regroup(mixed_up, lift_up)
    gelu_value, gelu_slope = gelu_pair(pre_act)
    activated = gelu_value.astype(jnp.bfloat16)
    down_four = down_first.reshape(local_blocks, hidden_size, NB, slice_width)
    mixed_down = jnp.einsum(
        "jmt,jmkc->jckt", activated, down_four, preferred_element_type=jnp.float32
    ).astype(jnp.bfloat16)

    def settle(received):
        regrouped = received.reshape(block_size, local_blocks, received.shape[3])
        return (
            regrouped,
            jnp.einsum("mkt,kmo->kot", regrouped, down_second, preferred_element_type=jnp.float32),
        )

    regrouped_down, branch = regroup(mixed_down, settle)
    branch_rows = branch.transpose(2, 0, 1).reshape(token_rows, local_blocks * block_size)
    layer_out = (tokens.astype(jnp.float32) + branch_rows).astype(jnp.bfloat16)
    grad_three = cotangent.reshape(token_rows, local_blocks, block_size)
    last_four = down_second.reshape(local_blocks, NB, slice_width, block_size)
    back_down = jnp.einsum(
        "tko,kjco->kcjt", grad_three, last_four, preferred_element_type=jnp.float32
    ).astype(jnp.bfloat16)

    def descend(received):
        regrouped = received.reshape(block_size, local_blocks, received.shape[3])
        return (
            regrouped,
            jnp.einsum("ojt,jmo->jmt", regrouped, down_first, preferred_element_type=jnp.float32),
        )

    grad_mid, grad_act = regroup(back_down, descend)
    grad_pre = (grad_act * gelu_slope).astype(jnp.bfloat16)
    term_fourth = grad_scale * jnp.einsum(
        "mkt,tko->mko", regrouped_down, grad_three, preferred_element_type=jnp.float32
    )
    term_third = grad_scale * jnp.einsum(
        "jmt,ojt->mjo", activated, grad_mid, preferred_element_type=jnp.float32
    )
    up_back = up_second.reshape(local_blocks, NB, slice_width, hidden_size)
    back_up = jnp.einsum(
        "jot,jbco->jcbt", grad_pre, up_back, preferred_element_type=jnp.float32
    ).astype(jnp.bfloat16)

    def arrive(received):
        regrouped = received.reshape(block_size, local_blocks, received.shape[3])
        return (
            regrouped,
            jnp.einsum("obt,bio->bit", regrouped, up_first, preferred_element_type=jnp.float32),
        )

    grad_in, back_branch = regroup(back_up, arrive)
    back_rows = back_branch.transpose(2, 0, 1).reshape(token_rows, local_blocks * block_size)
    grad_tokens = (cotangent.astype(jnp.float32) + back_rows).astype(jnp.bfloat16)
    term_second = grad_scale * jnp.einsum(
        "mjt,jot->mjo", regrouped_up, grad_pre, preferred_element_type=jnp.float32
    )
    term_first = grad_scale * jnp.einsum(
        "tbi,obt->ibo", x_three, grad_in, preferred_element_type=jnp.float32
    )
    sum_first, sum_second, sum_third, sum_fourth = (
        lax.psum_scatter(
            term_first.astype(jnp.bfloat16), "dp", scatter_dimension=0, tiled=True
        ).astype(jnp.float32),
        lax.psum_scatter(
            term_second.astype(jnp.bfloat16), "dp", scatter_dimension=0, tiled=True
        ).astype(jnp.float32),
        lax.psum_scatter(
            term_third.astype(jnp.bfloat16), "dp", scatter_dimension=0, tiled=True
        ).astype(jnp.float32),
        lax.psum_scatter(
            term_fourth.astype(jnp.bfloat16), "dp", scatter_dimension=0, tiled=True
        ).astype(jnp.float32),
    )
    grad_up_first = sum_first.transpose(1, 0, 2)
    grad_up_second = sum_second.transpose(1, 0, 2)
    grad_down_first = sum_third.transpose(1, 0, 2)
    grad_down_second = sum_fourth.transpose(1, 0, 2)
    return (
        layer_out,
        grad_tokens,
        grad_up_first,
        grad_up_second,
        grad_down_first,
        grad_down_second,
    )


def solution(mesh):
    in_specs = (
        P("dp", "tensor"),
        P("tensor", None, None),
        P("tensor", None, None),
        P("tensor", None, None),
        P("tensor", None, None),
        P("dp", "tensor"),
    )
    out_specs = (
        P("dp", "tensor"),
        P("dp", "tensor"),
        P("tensor", "dp", None),
        P("tensor", "dp", None),
        P("tensor", "dp", None),
        P("tensor", "dp", None),
    )
    return jax.shard_map(body, mesh=mesh, in_specs=in_specs, out_specs=out_specs, check_vma=False)
```

profile of v0, /device:TPU:0, one launch (start us, length us, event | category | flops | bytes accessed | tf_op | source)
XLA Modules:
  0.0 465.9 jit_solution(12066908594046687807)
XLA Ops:
  7.2 4.0 reshape.59
  11.2 2.7 fusion.30
  13.9 1.4 copy.105
  15.3 6.3 %all-to-all-start.2 = ((bf16[4,32,16,384]{3,1,0,2:T(8,128)(2,1)}), bf16[4,32,16,384]{3,1,0,2:T(8,128)(2,1)}, u32[]{:S(2)}, u32[]{:S(2)}) async-start(bf16[4,32,16,384]{3,1,0,2:T(8,128)(2,1)} %copy.105), calls=%async_computation.2 | async-start | bytes 3145728 | tf_op jit(solution)/shard_map/all_to_all | solution.py:22
  21.6 3.8 reshape.53
  25.4 4.1 copy.90
  29.6 3.3 fusion.27
  32.9 1.4 copy.92
  34.3 24.4 %all-to-all-done.2 = bf16[4,32,16,384]{3,1,0,2:T(8,128)(2,1)} async-done(((bf16[4,32,16,384]{3,1,0,2:T(8,128)(2,1)}), bf16[4,32,16,384]{3,1,0,2:T(8,128)(2,1)}, u32[]{:S(2)}, u32[]{:S(2)}) %all-to-all-start.2) | async-done | bytes 1572896 | tf_op jit(solution)/shard_map/all_to_all | solution.py:22
  58.7 4.4 all-to-all-start
  63.0 2.8 copy.107
  65.8 33.7 %all-to-all-done = bf16[4,32,16,384]{3,1,0,2:T(8,128)(2,1)} async-done(((bf16[4,32,16,384]{3,1,0,2:T(8,128)(2,1)}), bf16[4,32,16,384]{3,1,0,2:T(8,128)(2,1)}, u32[]{:S(2)}, u32[]{:S(2)}) %all-to-all-start) | async-done | bytes 1572896 | tf_op jit(solution)/shard_map/all_to_all | solution.py:22
  99.5 1.6 copy.94
  102.3 6.0 %fusion.34 = f32[4,384,2048]{2,1,0:T(8,128)S(1)} fusion(bf16[512,4,384]{2,0,1:T(8,128)(2,1)S(1)} %bitcast.120, bf16[4,512,2048]{2,1,0:T(8,128)(2,1)} %param.8), kind=kOutput, calls=%fused_computation.45 | convolution fusion | flops 3221225472 | bytes 22544384 | tf_op jit(solution)/shard_map/mjt,jmo->jot/dot_general | solution.py:43
  108.3 11.5 %fusion.33 = f32[4,384,512]{1,2,0:S(1)} fusion(bf16[4,2048,512]{2,1,0:T(8,128)(2,1)} %param.9, f32[4,384,2048]{2,1,0:T(8,128)S(1)} %fusion.34), kind=kOutput, calls=%fused_computation.44 | convolution fusion | flops 3249537024 | bytes 24117248
  120.0 1.4 copy.98
  121.4 4.3 all-to-all-start.1
  126.3 16.0 %fusion.6 = bf16[4,2048,384]{1,2,0:T(8,128)(2,1)} fusion(f32[4,384,2048]{2,1,0:T(8,128)} %copy-done.1, bf16[512,4,384]{2,0,1:T(8,128)(2,1)} %bitcast.124, bf16[4,2048,512]{2,1,0:T(8,128)(2,1)} %param.9), kind=kOutput, calls=%fused_computation.10 | convolution fusion | flops 3280994304 | bytes 28835840 | tf_op jit(solution)/shard_map/ojt,jmo->jmt/dot_general | solution.py:74
  142.3 20.0 %all-to-all-done.1 = bf16[4,32,16,384]{3,1,0,2:T(8,128)(2,1)} async-done(((bf16[4,32,16,384]{3,1,0,2:T(8,128)(2,1)}), bf16[4,32,16,384]{3,1,0,2:T(8,128)(2,1)}, u32[]{:S(2)}, u32[]{:S(2)}) %all-to-all-start.1) | async-done | bytes 1572896 | tf_op jit(solution)/shard_map/all_to_all | solution.py:22
  162.3 1.7 copy.100
  165.1 2.6 fusion.17
  167.7 9.9 %fusion.24 = bf16[4,32,16,384]{3,1,2,0:T(8,128)(2,1)S(1)} fusion(bf16[4,16,32,2048]{3,2,1,0:T(8,128)(2,1)} %bitcast.113, bf16[4,2048,384]{1,2,0:T(8,128)(2,1)} %fusion.6), kind=kOutput, calls=%fused_computation.39 | convolution fusion | flops 3222011904 | bytes 16252928 | tf_op jit(solution)/shard_map/jot,jbco->jcbt/dot_general | solution.py:86
  177.6 1.4 copy.110
  179.0 4.4 all-to-all-start.3
  183.6 11.6 %fusion.7 = bf16[512,4,2048]{0,2,1:T(8,128)(2,1)} fusion(bf16[4,2048,384]{1,2,0:T(8,128)(2,1)} %fusion.6, bf16[512,4,384]{2,0,1:T(8,128)(2,1)} %bitcast.121), kind=kOutput, calls=%fused_computation.13 | convolution fusion | flops 3229614080 | bytes 16252928 | tf_op jit(solution)/shard_map/mjt,jot->mjo/dot_general | solution.py:100
  195.2 14.9 %copy.118 = bf16[512,4,2048]{2,1,0:T(4,128)(2,1)} copy(bf16[512,4,2048]{0,2,1:T(8,128)(2,1)} %fusion.7) | data formatting | bytes 16777216 | tf_op jit(solution)/shard_map/convert_element_type | solution.py:111
  210.1 9.6 %all-to-all-done.3 = bf16[4,32,16,384]{3,1,0,2:T(8,128)(2,1)} async-done(((bf16[4,32,16,384]{3,1,0,2:T(8,128)(2,1)}), bf16[4,32,16,384]{3,1,0,2:T(8,128)(2,1)}, u32[]{:S(2)}, u32[]{:S(2)}) %all-to-all-start.3) | async-done | bytes 1572896 | tf_op jit(solution)/shard_map/all_to_all | solution.py:22
  219.7 1.7 copy.112
  222.6 2.6 fusion.16
  225.2 4.5 copy.116
  229.9 11.0 %fusion.8 = bf16[2048,4,512]{0,2,1:T(8,128)(2,1)} fusion(bf16[512,4,384]{2,0,1:T(8,128)(2,1)} %bitcast.125, f32[4,384,2048]{2,1,0:T(8,128)} %copy-done.1), kind=kOutput, calls=%fused_computation.14 | convolution fusion | flops 3257925632 | bytes 22544384 | tf_op jit(solution)/shard_map/jmt,ojt->mjo/dot_general | solution.py:82
  241.0 2.6 copy.89
  243.6 2.6 copy.103
  247.4 4.1 convolution_bitcast_fusion.1
  251.5 3.6 copy.102
  255.1 4.1 fusion.12
  259.2 2.7 copy.121
  261.9 4.9 %convolution_bitcast_fusion = f32[384,4,512]{2,0,1:T(8,128)} fusion(bf16[512,4,384]{2,0,1:T(8,128)(2,1)} %bitcast.119, bf16[4,512,512]{2,1,0:T(8,128)(2,1)} %param.7), kind=kOutput, calls=%fused_computation.25 | convolution fusion | flops 805306368 | bytes 6815744 | tf_op jit(solution)/shard_map/obt,bio->bit/dot_general | solution.py:94
  266.9 3.6 copy.114
  270.5 3.9 fusion.11
  274.4 2.6 copy.122
  277.1 1.8 convert_bitcast_fusion.3
  278.9 99.8 %all-reduce.5.cloned.1.call-done = (bf16[512,4,512]{2,1,0:T(4,128)(2,1)}, bf16[512,4,2048]{2,1,0:T(4,128)(2,1)}) async-done(((bf16[512,4,512]{2,1,0:T(4,128)(2,1)}, bf16[512,4,2048]{2,1,0:T(4,128)(2,1)}), (bf16[512,4,512]{2,1,0:T(4,128)(2,1)}, bf16[512,4,2048]{2,1,0:T(4,128)(2,1)})) %all-reduce.5.cloned.1.call-update) | async-done | bytes 10485776
  378.7 1.4 convert_bitcast_fusion.1
  380.1 2.5 copy.124
  384.6 69.0 %reduce-scatter.3.cloned.1.call-done = bf16[256,4,512]{0,2,1:T(8,128)(2,1)} async-done(((bf16[2048,4,512]{0,2,1:T(8,128)(2,1)}), bf16[256,4,512]{0,2,1:T(8,128)(2,1)}) %reduce-scatter.3.cloned.1.call-update) | async-done | bytes 1048592 | tf_op jit(solution)/shard_map/reduce_scatter | solution.py:113
  453.5 2.7 convert_bitcast_fusion
  456.3 2.9 copy.125
  (27 shorter events, 7.2 us)
Async XLA Ops:
  7.2 4.0 copy-start
  15.3 43.4 %all-to-all-start.2 = ((bf16[4,32,16,384]{3,1,0,2:T(8,128)(2,1)}), bf16[4,32,16,384]{3,1,0,2:T(8,128)(2,1)}, u32[]{:S(2)}, u32[]{:S(2)}) async-start(bf16[4,32,16,384]{3,1,0,2:T(8,128)(2,1)} %copy.105), calls=%async_computation.2 | async-start | bytes 3145728 | tf_op jit(solution)/shard_map/all_to_all | solution.py:22
  58.7 40.9 %all-to-all-start = ((bf16[4,32,16,384]{3,1,0,2:T(8,128)(2,1)}), bf16[4,32,16,384]{3,1,0,2:T(8,128)(2,1)}, u32[]{:S(2)}, u32[]{:S(2)}) async-start(bf16[4,32,16,384]{3,1,0,2:T(8,128)(2,1)} %copy.92), calls=%async_computation | async-start | bytes 3145728 | tf_op jit(solution)/shard_map/all_to_all | solution.py:22
  101.2 1.1 copy-start.6
  108.3 11.5 %copy-start.1 = (f32[4,384,2048]{2,1,0:T(8,128)}, f32[4,384,2048]{2,1,0:T(8,128)S(1)}, u32[]{:S(2)}) copy-start(f32[4,384,2048]{2,1,0:T(8,128)S(1)} %fusion.34) | copy-start | bytes 37748740
  121.4 40.9 %all-to-all-start.1 = ((bf16[4,32,16,384]{3,1,0,2:T(8,128)(2,1)}), bf16[4,32,16,384]{3,1,0,2:T(8,128)(2,1)}, u32[]{:S(2)}, u32[]{:S(2)}) async-start(bf16[4,32,16,384]{3,1,0,2:T(8,128)(2,1)} %copy.98), calls=%async_computation.1 | async-start | bytes 3145728 | tf_op jit(solution)/shard_map/all_to_all | solution.py:22
  125.8 151.3 %reduce-scatter.5.cloned.1.call-start = ((), (), s32[]{:S(2)}) async-start(), calls=%async_computation.7 | async-start | bytes 2359296 | tf_op jit(solution)/shard_map/reduce_scatter | solution.py:116
  162.3 2.8 copy-start.3
  164.0 1.1 copy-start.4
  179.0 40.7 %all-to-all-start.3 = ((bf16[4,32,16,384]{3,1,0,2:T(8,128)(2,1)}), bf16[4,32,16,384]{3,1,0,2:T(8,128)(2,1)}, u32[]{:S(2)}, u32[]{:S(2)}) async-start(bf16[4,32,16,384]{3,1,0,2:T(8,128)(2,1)} %copy.110), calls=%async_computation.3 | async-start | bytes 3145728 | tf_op jit(solution)/shard_map/all_to_all | solution.py:22
  183.4 195.3 %all-reduce.5.cloned.1.call-start = ((), (), s32[]{:S(2)}) async-start(), calls=%async_computation.8 | async-start | bytes 20971520
  219.7 2.9 copy-start.2
  221.4 1.2 copy-start.5
  229.7 223.9 %reduce-scatter.3.cloned.1.call-start = ((), (), s32[]{:S(2)}) async-start(), calls=%async_computation.6 | async-start | bytes 9437184 | tf_op jit(solution)/shard_map/reduce_scatter | solution.py:113
  241.0 5.2 %copy-start.7 = (u32[32]{0:T(128)S(1)}, u32[32]{0:T(128)}, u32[]{:S(2)}) copy-start(u32[32]{0:T(128)} %constant.16) | copy-start | bytes 388
Sparse Core Ops, SparseCore 0:
  167.8 40.3 reduce-scatter.4
  229.8 148.8 all-reduce.4
  382.1 71.3 reduce-scatter.2
where the time goes:
time: 474 us; the launch traced here: 466 us
  waiting for transfers between devices  257 us (54%)
  matrix products  86 us (18%)
  local copies, waits for them, and re-layouts  73 us (15%)
  starting transfers between devices  20.3 us (4%)
  other arithmetic  15.2 us (3%)
  between operations  14.8 us (3%)
    unnamed x4, waiting for transfers between devices  99.8 us
    all_to_all x4, waiting for transfers between devices, regroup(): lax.all_to_all(sliced, 'tensor', split_axis=2, concat_axis=0, tiled=True)  87.7 us
    reduce_scatter x1, waiting for transfers between devices, body(): lax.psum_scatter(term_third.astype(jnp.bfloat16), 'dp', scatter_dimension...  69 us
    unnamed x25, local copies, waits for them, and re-layouts  25.1 us
    all_to_all x4, starting transfers between devices, regroup(): lax.all_to_all(sliced, 'tensor', split_axis=2, concat_axis=0, tiled=True)  19.4 us
    dot_general x1, matrix products, descend(): jnp.einsum('ojt,jmo->jmt', regrouped, down_first, preferred_element_type=...  16 us
    convert_element_type x1, local copies, waits for them, and re-layouts, body(): term_second.astype(jnp.bfloat16)  14.9 us
    dot_general x1, matrix products, body(): jnp.einsum('mjt,jot->mjo', regrouped_up, grad_pre, preferred_element_type...  11.6 us
  transfers between devices with their start and end apart: 7, of which 6 were waited for; matrix products, arithmetic and copies ran while one was open for 28% of the time, Pallas kernels for 0%

commit v1 on v0

--- a/solution.py
+++ b/solution.py
@@ -19,7 +19,14 @@
 
 
 def regroup(sliced, apply_fn):
-    return apply_fn(lax.all_to_all(sliced, "tensor", split_axis=2, concat_axis=0, tiled=True))
+    return apply_fn(
+        jnp.concatenate(
+            jax.lax.all_to_all(
+                jnp.stack(jnp.split(sliced, jax.lax.axis_size("tensor"), 2), 0), "tensor", 0, 0
+            ),
+            0,
+        )
+    )
 
 
 def body(tokens, up_first, up_second, down_first, down_second, cotangent):

time: 474 us -> 458 us (0.966)
  waiting for transfers between devices: 257 us -> 237 us
  other arithmetic: 15.2 us -> 20.8 us
    all_to_all x4, waiting for transfers between devices: 87.7 us -> 68.5 us  [regroup(): jax.lax.all_to_all(jnp.stack(jnp.split(sliced, jax.lax.axis_size('tensor'...]
    convert_element_type x4 -> x0, local copies, waits for them, and re-layouts: 5.58 us -> none  [the longest x1 1.41 us: body(): mixed_down = jnp.einsum('jmt,jmkc->jckt', activated, down_four, preferred...]
    another operation x0 -> x4, other arithmetic: none -> 5.55 us  [regroup(): jnp.stack(jnp.split(sliced, jax.lax.axis_size('tensor'), 2), 0)]
    unnamed x25 -> x27, local copies, waits for them, and re-layouts: 25.1 us -> 26.2 us
  transfers between devices with their start and end apart: 7 -> 7, of which waited for: 6 -> 6; matrix products, arithmetic and copies ran while one was open for 28% -> 33% of each run, Pallas kernels for 0% -> 0%
where the time goes in v1:
time: 458 us; the launch traced here: 449 us
  waiting for transfers between devices  237 us (52%)
  matrix products  87.6 us (19%)
  local copies, waits for them, and re-layouts  68.3 us (15%)
  other arithmetic  20.8 us (5%)
  starting transfers between devices  20.4 us (4%)
  between operations  14.9 us (3%)
    unnamed x4, waiting for transfers between devices  99.9 us
    reduce_scatter x1, waiting for transfers between devices, body(): lax.psum_scatter(term_third.astype(jnp.bfloat16), 'dp', scatter_dimension...  69 us
    all_to_all x4, waiting for transfers between devices, regroup(): jax.lax.all_to_all(jnp.stack(jnp.split(sliced, jax.lax.axis_size('tensor'...  68.5 us
    unnamed x27, local copies, waits for them, and re-layouts  26.2 us
    all_to_all x4, starting transfers between devices, regroup(): jax.lax.all_to_all(jnp.stack(jnp.split(sliced, jax.lax.axis_size('tensor'...  19.4 us
    dot_general x1, matrix products, descend(): jnp.einsum('ojt,jmo->jmt', regrouped, down_first, preferred_element_type=...  17.6 us
    convert_element_type x1, local copies, waits for them, and re-layouts, body(): term_second.astype(jnp.bfloat16)  14.9 us
    dot_general x1, matrix products, body(): jnp.einsum('mjt,jot->mjo', regrouped_up, grad_pre, preferred_element_type...  11.5 us
  transfers between devices with their start and end apart: 7, of which 6 were waited for; matrix products, arithmetic and copies ran while one was open for 33% of the time, Pallas kernels for 0%

profile of v1, /device:TPU:0, one launch (start us, length us, event | category | flops | bytes accessed | tf_op | source)
XLA Modules:
  0.0 449.3 jit_solution(3907767843011793881)
XLA Ops:
  7.2 4.0 reshape.37
  11.2 4.1 copy.57
  15.3 3.3 fusion.27
  18.9 1.4 pad_maximum_fusion
  20.3 6.3 %all-to-all-start = ((bf16[4,4,32,4,384]{4,2,3,1,0:T(8,128)(2,1)}), bf16[4,4,32,4,384]{4,2,3,1,0:T(8,128)(2,1)}, u32[]{:S(2)}, u32[]{:S(2)}) async-start(bf16[4,4,32,4,384]{4,2,3,1,0:T(8,128)(2,1)} %pad_maximum_fusion), calls=%async_computation | async-start | bytes 3145728 | tf_op jit(solution)/shard_map/all_to_all | solution.py:24
  26.6 3.8 reshape.41
  30.4 2.7 fusion.30
  33.4 1.4 pad_maximum_fusion.2
  34.8 28.9 %all-to-all-done = bf16[4,4,32,4,384]{4,2,3,1,0:T(8,128)(2,1)} async-done(((bf16[4,4,32,4,384]{4,2,3,1,0:T(8,128)(2,1)}), bf16[4,4,32,4,384]{4,2,3,1,0:T(8,128)(2,1)}, u32[]{:S(2)}, u32[]{:S(2)}) %all-to-all-start) | async-done | bytes 1572896 | tf_op jit(solution)/shard_map/all_to_all | solution.py:24
  63.7 4.4 all-to-all-start.2
  68.0 1.7 copy.59
  70.9 6.0 %fusion.34 = f32[4,384,2048]{2,1,0:T(8,128)S(1)} fusion(bf16[512,4,384]{2,0,1:T(8,128)(2,1)S(1)} %bitcast.140, bf16[4,512,2048]{2,1,0:T(8,128)(2,1)} %param.8), kind=kOutput, calls=%fused_computation.65 | convolution fusion | flops 3221225472 | bytes 22544384 | tf_op jit(solution)/shard_map/mjt,jmo->jot/dot_general | solution.py:50
  76.8 11.5 %fusion.33 = f32[4,384,512]{1,2,0:S(1)} fusion(bf16[4,2048,512]{2,1,0:T(8,128)(2,1)} %param.9, f32[4,384,2048]{2,1,0:T(8,128)S(1)} %fusion.34), kind=kOutput, calls=%fused_computation.64 | convolution fusion | flops 3249537024 | bytes 24117248
  88.7 1.4 pad_maximum_fusion.1
  90.1 14.5 %all-to-all-done.2 = bf16[4,4,32,4,384]{4,2,3,1,0:T(8,128)(2,1)} async-done(((bf16[4,4,32,4,384]{4,2,3,1,0:T(8,128)(2,1)}), bf16[4,4,32,4,384]{4,2,3,1,0:T(8,128)(2,1)}, u32[]{:S(2)}, u32[]{:S(2)}) %all-to-all-start.2) | async-done | bytes 1572896 | tf_op jit(solution)/shard_map/all_to_all | solution.py:24
  104.6 4.4 all-to-all-start.1
  109.4 1.7 copy.68
  112.3 17.6 %fusion.6 = bf16[4,2048,384]{1,2,0:T(8,128)(2,1)} fusion(f32[4,384,2048]{2,1,0:T(8,128)} %copy-done.1, bf16[512,4,384]{2,0,1:T(8,128)(2,1)S(1)} %bitcast.144, bf16[4,2048,512]{2,1,0:T(8,128)(2,1)} %param.9), kind=kOutput, calls=%fused_computation.10 | convolution fusion | flops 3280994304 | bytes 28835840 | tf_op jit(solution)/shard_map/ojt,jmo->jmt/dot_general | solution.py:81
  129.9 15.5 %all-to-all-done.1 = bf16[4,4,32,4,384]{4,2,3,1,0:T(8,128)(2,1)} async-done(((bf16[4,4,32,4,384]{4,2,3,1,0:T(8,128)(2,1)}), bf16[4,4,32,4,384]{4,2,3,1,0:T(8,128)(2,1)}, u32[]{:S(2)}, u32[]{:S(2)}) %all-to-all-start.1) | async-done | bytes 1572896 | tf_op jit(solution)/shard_map/all_to_all | solution.py:24
  145.4 1.8 copy.63
  148.4 2.6 fusion.17
  150.9 9.9 %fusion.24 = bf16[4,32,16,384]{3,1,2,0:T(8,128)(2,1)S(1)} fusion(bf16[4,16,32,2048]{3,2,1,0:T(8,128)(2,1)} %bitcast.133, bf16[4,2048,384]{1,2,0:T(8,128)(2,1)} %fusion.6), kind=kOutput, calls=%fused_computation.43 | convolution fusion | flops 3222011904 | bytes 16252928 | tf_op jit(solution)/shard_map/jot,jbco->jcbt/dot_general | solution.py:93
  161.0 1.4 pad_maximum_fusion.3
  162.4 4.4 all-to-all-start.3
  167.0 11.5 %fusion.7 = bf16[512,4,2048]{0,2,1:T(8,128)(2,1)} fusion(bf16[4,2048,384]{1,2,0:T(8,128)(2,1)} %fusion.6, bf16[512,4,384]{2,0,1:T(8,128)(2,1)} %bitcast.141), kind=kOutput, calls=%fused_computation.13 | convolution fusion | flops 3229614080 | bytes 16252928 | tf_op jit(solution)/shard_map/mjt,jot->mjo/dot_general | solution.py:107
  178.5 14.9 %copy.77 = bf16[512,4,2048]{2,1,0:T(4,128)(2,1)} copy(bf16[512,4,2048]{0,2,1:T(8,128)(2,1)} %fusion.7) | data formatting | bytes 16777216 | tf_op jit(solution)/shard_map/convert_element_type | solution.py:118
  193.4 9.7 %all-to-all-done.3 = bf16[4,4,32,4,384]{4,2,3,1,0:T(8,128)(2,1)} async-done(((bf16[4,4,32,4,384]{4,2,3,1,0:T(8,128)(2,1)}), bf16[4,4,32,4,384]{4,2,3,1,0:T(8,128)(2,1)}, u32[]{:S(2)}, u32[]{:S(2)}) %all-to-all-start.3) | async-done | bytes 1572896 | tf_op jit(solution)/shard_map/all_to_all | solution.py:24
  203.1 1.8 copy.71
  206.0 2.6 fusion.16
  208.6 4.5 copy.75
  213.3 10.9 %fusion.8 = bf16[2048,4,512]{0,2,1:T(8,128)(2,1)} fusion(bf16[512,4,384]{2,0,1:T(8,128)(2,1)} %bitcast.145, f32[4,384,2048]{2,1,0:T(8,128)} %copy-done.1), kind=kOutput, calls=%fused_computation.14 | convolution fusion | flops 3257925632 | bytes 22544384 | tf_op jit(solution)/shard_map/jmt,ojt->mjo/dot_general | solution.py:89
  224.3 2.6 copy.56
  226.9 2.6 copy.66
  230.7 4.1 convolution_bitcast_fusion.1
  234.8 3.6 copy.65
  238.4 4.1 fusion.12
  242.5 2.8 copy.80
  245.3 4.9 %convolution_bitcast_fusion = f32[384,4,512]{2,0,1:T(8,128)} fusion(bf16[512,4,384]{2,0,1:T(8,128)(2,1)} %bitcast.139, bf16[4,512,512]{2,1,0:T(8,128)(2,1)} %param.7), kind=kOutput, calls=%fused_computation.25 | convolution fusion | flops 805306368 | bytes 6815744 | tf_op jit(solution)/shard_map/obt,bio->bit/dot_general | solution.py:101
  250.2 3.6 copy.73
  253.8 3.9 fusion.11
  257.8 2.6 copy.81
  260.4 1.8 convert_bitcast_fusion.3
  262.2 99.8 %all-reduce.5.cloned.1.call-done = (bf16[512,4,512]{2,1,0:T(4,128)(2,1)}, bf16[512,4,2048]{2,1,0:T(4,128)(2,1)}) async-done(((bf16[512,4,512]{2,1,0:T(4,128)(2,1)}, bf16[512,4,2048]{2,1,0:T(4,128)(2,1)}), (bf16[512,4,512]{2,1,0:T(4,128)(2,1)}, bf16[512,4,2048]{2,1,0:T(4,128)(2,1)})) %all-reduce.5.cloned.1.call-update) | async-done | bytes 10485776
  362.0 1.4 convert_bitcast_fusion.1
  363.5 2.5 copy.83
  368.0 69.0 %reduce-scatter.3.cloned.1.call-done = bf16[256,4,512]{0,2,1:T(8,128)(2,1)} async-done(((bf16[2048,4,512]{0,2,1:T(8,128)(2,1)}), bf16[256,4,512]{0,2,1:T(8,128)(2,1)}) %reduce-scatter.3.cloned.1.call-update) | async-done | bytes 1048592 | tf_op jit(solution)/shard_map/reduce_scatter | solution.py:120
  436.9 2.7 convert_bitcast_fusion
  439.7 2.9 copy.84
  (33 shorter events, 9.1 us)
Async XLA Ops:
  7.2 23.3 %copy-start = (bf16[4,512,512]{2,1,0:T(8,128)(2,1)S(1)}, bf16[4,512,512]{2,1,0:T(8,128)(2,1)}, u32[]{:S(2)}) copy-start(bf16[4,512,512]{2,1,0:T(8,128)(2,1)} %param.10) | copy-start | bytes 6291460
  20.3 43.4 %all-to-all-start = ((bf16[4,4,32,4,384]{4,2,3,1,0:T(8,128)(2,1)}), bf16[4,4,32,4,384]{4,2,3,1,0:T(8,128)(2,1)}, u32[]{:S(2)}, u32[]{:S(2)}) async-start(bf16[4,4,32,4,384]{4,2,3,1,0:T(8,128)(2,1)} %pad_maximum_fusion), calls=%async_computation | async-start | bytes 3145728 | tf_op jit(solution)/shard_map/all_to_all | solution.py:24
  63.7 40.9 %all-to-all-start.2 = ((bf16[4,4,32,4,384]{4,2,3,1,0:T(8,128)(2,1)}), bf16[4,4,32,4,384]{4,2,3,1,0:T(8,128)(2,1)}, u32[]{:S(2)}, u32[]{:S(2)}) async-start(bf16[4,4,32,4,384]{4,2,3,1,0:T(8,128)(2,1)} %pad_maximum_fusion.2), calls=%async_computation.2 | async-start | bytes 3145728 | tf_op jit(solution)/shard_map/all_to_all | solution.py:24
  69.7 1.1 copy-start.6
  76.8 11.5 %copy-start.1 = (f32[4,384,2048]{2,1,0:T(8,128)}, f32[4,384,2048]{2,1,0:T(8,128)S(1)}, u32[]{:S(2)}) copy-start(f32[4,384,2048]{2,1,0:T(8,128)S(1)} %fusion.34) | copy-start | bytes 37748740
  104.6 40.9 %all-to-all-start.1 = ((bf16[4,4,32,4,384]{4,2,3,1,0:T(8,128)(2,1)}), bf16[4,4,32,4,384]{4,2,3,1,0:T(8,128)(2,1)}, u32[]{:S(2)}, u32[]{:S(2)}) async-start(bf16[4,4,32,4,384]{4,2,3,1,0:T(8,128)(2,1)} %pad_maximum_fusion.1), calls=%async_computation.1 | async-start | bytes 3145728 | tf_op jit(solution)/shard_map/all_to_all | solution.py:24
  108.9 151.5 %reduce-scatter.5.cloned.1.call-start = ((), (), s32[]{:S(2)}) async-start(), calls=%async_computation.7 | async-start | bytes 2359296 | tf_op jit(solution)/shard_map/reduce_scatter | solution.py:123
  111.1 1.2 copy-start.7
  145.4 2.9 copy-start.3
  147.2 1.1 copy-start.4
  162.4 40.7 %all-to-all-start.3 = ((bf16[4,4,32,4,384]{4,2,3,1,0:T(8,128)(2,1)}), bf16[4,4,32,4,384]{4,2,3,1,0:T(8,128)(2,1)}, u32[]{:S(2)}, u32[]{:S(2)}) async-start(bf16[4,4,32,4,384]{4,2,3,1,0:T(8,128)(2,1)} %pad_maximum_fusion.3), calls=%async_computation.3 | async-start | bytes 3145728 | tf_op jit(solution)/shard_map/all_to_all | solution.py:24
  166.7 195.3 %all-reduce.5.cloned.1.call-start = ((), (), s32[]{:S(2)}) async-start(), calls=%async_computation.8 | async-start | bytes 20971520
  203.1 2.9 copy-start.2
  204.9 1.1 copy-start.5
  213.1 223.9 %reduce-scatter.3.cloned.1.call-start = ((), (), s32[]{:S(2)}) async-start(), calls=%async_computation.6 | async-start | bytes 9437184 | tf_op jit(solution)/shard_map/reduce_scatter | solution.py:120
  226.9 2.6 copy-start.8
Sparse Core Ops, SparseCore 0:
  151.1 40.3 reduce-scatter.4
  213.2 148.8 all-reduce.4
  365.5 71.3 reduce-scatter.2
